TPU v7x, 32 devices: a whole 2x2x4 slice. The times are simulated.
32 devices in a mesh: sample: 2 (over y), harm: 16 (over z, x, core).
Axes of the slice: x: 2, y: 2, z: 4, core: 2. Of those that a mesh axis runs over, the one named last changes fastest.
Arguments:
- inputs: bfloat16 [128, 64, 512], P('sample', 'harm'), parts along dimension 0, may hold values from -6 to 6
- col_list: int32 [128], P('sample'), parts along dimension 0, may hold values from 0 to 63, each once
- row_list: int32 [128], P('sample'), parts along dimension 0, may hold values from 0 to 63, each once
- gain_attn: float32 [512], replicated, may hold values from 0.25 to 1.75
- w_qkv: bfloat16 [512, 1536], replicated
- w_out: bfloat16 [512, 512], replicated, may hold values from -0.25 to 0.25
- gain_ffn: float32 [512], replicated, may hold values from 0.25 to 1.75
- w_gate: bfloat16 [512, 1024], P('harm'), may hold values from -0.25 to 0.25
- w_up: bfloat16 [512, 1024], P('harm'), may hold values from -0.25 to 0.25
- w_down: bfloat16 [1024, 512], P('harm'), may hold values from -0.1875 to 0.1875
Outputs:
- result: bfloat16 [64, 128, 512], P('harm', 'sample'), parts along dimension 1
There are 2 independent parts, one for each index of `sample`. A program takes and returns all parts, laid end to end along the dimension named above; an argument that names none is the same for every part. Nothing has to cross between parts.
Inputs may be any that keep to these rules, and one draw needn't show every extreme that they name: col_list names every order m of 0 to 63 exactly once. row_list names every degree ell of 0 to 63 exactly once.
All inputs are finite; a program needn't handle non-finite values.
Results may differ from a plain program's by a relative error of at most 0.0073.
Values may be sent and summed in bfloat16 or wider, within the bound.
A program may use at most 64 MiB of HBM per device.

v0:
```python
import jax
import jax.numpy as jnp
from jax import lax
from jax.sharding import PartitionSpec as P

HEADS = 8
WIN = 256
eps = 1e-06
masked = -1e30


def rms_scale(values, gain):
    values = values.astype(jnp.float32)
    mean_sq = jnp.mean(values * values, axis=-1, keepdims=True)
    return values * lax.rsqrt(mean_sq + eps) * gain


def split_heads(block, start, split, head_dim):
    piece = block[..., start : start + split]
    return piece.reshape(piece.shape[:-1] + (split // head_dim, head_dim))


def softmax_rounded(scores):
    top = jnp.max(scores, axis=-1, keepdims=True)
    weights = jnp.exp(scores - top)
    return (weights / jnp.sum(weights, axis=-1, keepdims=True)).astype(jnp.bfloat16)


def column_attention(query, keys, values, starts, scale):
    length = query.shape[0]
    here = jnp.arange(length, dtype=jnp.int32)
    offset = here[None, :] - here[:, None]
    band = (offset >= -(WIN // 2)) & (offset < WIN // 2)
    allowed = band[None] & (here[None, None, :] >= starts[:, None, None])
    scores = jnp.einsum("lchd,kchd->chlk", query, keys, preferred_element_type=jnp.float32) * scale
    scores = jnp.where(allowed[:, None], scores, masked)
    probs = softmax_rounded(scores)
    mixed = jnp.einsum("chlk,kchd->lchd", probs, values, preferred_element_type=jnp.float32)
    return mixed.astype(jnp.bfloat16)


def row_attention(query, keys, values, marks, limits, scale):
    diff = marks[None, :] - marks[:, None]
    band = (diff >= -(WIN // 2)) & (diff < WIN // 2)
    allowed = band[None] & (marks[None, None, :] <= limits[:, None, None])
    scores = jnp.einsum("ishd,ithd->ihst", query, keys, preferred_element_type=jnp.float32) * scale
    scores = jnp.where(allowed[:, None], scores, masked)
    probs = softmax_rounded(scores)
    mixed = jnp.einsum("ihst,ithd->ishd", probs, values, preferred_element_type=jnp.float32)
    return mixed.astype(jnp.bfloat16)


def per_device(inputs, col_list, row_list, gain_attn, w_qkv, w_out, gain_ffn, w_gate, w_up, w_down):
    place = lax.axis_index("harm")
    groups = lax.axis_size("harm")
    length, cols, width = inputs.shape
    rows_here = length // groups
    head_dim = width // HEADS
    half = HEADS // 2
    split = half * head_dim
    scale = head_dim ** (-0.5)
    my_cols = lax.dynamic_slice_in_dim(col_list, place * cols, cols)
    my_rows = lax.dynamic_slice_in_dim(row_list, place * rows_here, rows_here)
    gate_full, up_full, down_full = (
        lax.all_gather(w_gate, "harm", axis=0, tiled=True),
        lax.all_gather(w_up, "harm", axis=0, tiled=True),
        lax.all_gather(w_down, "harm", axis=0, tiled=True),
    )
    normed = rms_scale(inputs, gain_attn).astype(jnp.bfloat16)
    flat = normed.reshape(length * cols, width)
    qkv = jnp.dot(flat, w_qkv, preferred_element_type=jnp.float32)
    qkv = qkv.astype(jnp.bfloat16).reshape(length, cols, 3 * width)
    a_ell = column_attention(
        split_heads(qkv, 0, split, head_dim),
        split_heads(qkv, width, split, head_dim),
        split_heads(qkv, 2 * width, split, head_dim),
        my_cols,
        scale,
    )
    a_ell = a_ell.reshape(length, cols, split)
    feat_rows = jnp.take(inputs, row_list, axis=0)
    ell_rows = jnp.take(a_ell, row_list, axis=0)
    query_rows = jnp.take(qkv[:, :, split:width], row_list, axis=0)
    key_rows = jnp.take(qkv[:, :, width + split : 2 * width], row_list, axis=0)
    value_rows = jnp.take(qkv[:, :, 2 * width + split :], row_list, axis=0)
    feat_here, ell_here, query_here, key_here, value_here = (
        lax.all_to_all(feat_rows, "harm", split_axis=0, concat_axis=1, tiled=True),
        lax.all_to_all(ell_rows, "harm", split_axis=0, concat_axis=1, tiled=True),
        lax.all_to_all(query_rows, "harm", split_axis=0, concat_axis=1, tiled=True),
        lax.all_to_all(key_rows, "harm", split_axis=0, concat_axis=1, tiled=True),
        lax.all_to_all(value_rows, "harm", split_axis=0, concat_axis=1, tiled=True),
    )
    shape_heads = (rows_here, length, half, head_dim)
    a_m = row_attention(
        query_here.reshape(shape_heads),
        key_here.reshape(shape_heads),
        value_here.reshape(shape_heads),
        col_list,
        my_rows,
        scale,
    )
    attn = jnp.concatenate([ell_here, a_m.reshape(rows_here, length, split)], axis=-1)
    tokens = rows_here * length
    resid = feat_here.astype(jnp.float32).reshape(tokens, width) + jnp.dot(
        attn.reshape(tokens, width), w_out, preferred_element_type=jnp.float32
    )
    normed_ffn = rms_scale(resid, gain_ffn).astype(jnp.bfloat16)
    gate = jnp.dot(normed_ffn, gate_full, preferred_element_type=jnp.float32)
    up = jnp.dot(normed_ffn, up_full, preferred_element_type=jnp.float32)
    hidden = (jax.nn.silu(gate) * up).astype(jnp.bfloat16)
    final = (resid + jnp.dot(hidden, down_full, preferred_element_type=jnp.float32)).reshape(
        rows_here, length, width
    )
    valid = col_list[None, :] <= my_rows[:, None]
    return jnp.where(valid[:, :, None], final, 0.0).astype(jnp.bfloat16)


def solution(mesh):
    placed = (
        P("sample", "harm", None),
        P("sample"),
        P("sample"),
        P(),
        P(),
        P(),
        P(),
        P("harm", None),
        P("harm", None),
        P("harm", None),
    )
    return jax.shard_map(
        per_device, mesh=mesh, in_specs=placed, out_specs=P("harm", "sample", None), check_vma=False
    )
```

profile of v0, /device:TPU:0, one launch (start us, length us, event | category | flops | bytes accessed | tf_op | source)
XLA Modules:
  0.0 141.0 jit_solution(10194991990076802420)
XLA Ops:
  6.5 0.0 copy-start
  6.5 0.0 all-gather.4.cloned.1.call-start
  6.5 0.7 all-gather.4.cloned.1.call-update
  7.3 0.0 all-gather.6.cloned.1.call-start
  7.3 0.7 all-gather.6.cloned.1.call-update
  8.0 0.7 dynamic_slice.7
  8.8 0.1 iota_compare_fusion
  8.8 1.2 fusion.15
  10.0 1.2 fusion.17
  11.2 0.1 reshape.198
  11.2 0.0 copy-done
  11.3 0.6 convolution_convert_fusion
  11.8 0.2 reshape.199
  12.0 0.3 fusion.44
  12.3 0.1 broadcast_and_fusion.1
  12.4 0.2 reshape.263
  12.6 0.2 reshape.264
  12.8 0.2 copy.68
  13.0 0.3 fusion.8
  13.3 0.1 fusion.45
  13.4 0.0 copy-start.4
  13.4 0.3 convolution_convert_fusion.2
  13.7 0.2 copy.74
  13.9 0.2 copy-done.4
  14.1 0.7 gather_fusion.1
  14.8 0.0 copy-start.1
  14.8 0.7 gather_fusion.2
  15.5 0.7 gather_fusion.3
  16.2 0.7 gather_fusion.4
  16.9 1.1 broadcast_select_fusion.4
  18.0 15.5 %all_to_all.69 = bf16[64,4,256]{2,1,0:T(4,128)(2,1)S(1)} all-to-all(bf16[64,4,256]{2,1,0:T(4,128)(2,1)S(1)} %get-tuple-element.14), channel_id=1, replica_groups=mesh['sample'=2,'harm'=16] {'harm'}, dimensions={0} | all-to-all | bytes 262144 | tf_op jit(solution)/shard_map/all_to_all | solution.py:89
  33.5 3.5 %all-to-all-start.4 = ((bf16[64,4,256]{2,1,0:T(4,128)(2,1)}), bf16[64,4,256]{2,1,0:T(4,128)(2,1)S(1)}, u32[]{:S(2)}, u32[]{:S(2)}) async-start(bf16[64,4,256]{2,1,0:T(4,128)(2,1)} %get-tuple-element.15), calls=%async_computation.4 | async-start | bytes 262144 | tf_op jit(solution)/shard_map/all_to_all | solution.py:90
  37.0 0.0 all-gather.8.cloned.1.call-start
  37.0 0.7 all-gather.8.cloned.1.call-update
  37.7 0.1 dynamic_slice.6
  37.8 8.1 %all-to-all-done.4 = bf16[64,4,256]{2,1,0:T(4,128)(2,1)S(1)} async-done(((bf16[64,4,256]{2,1,0:T(4,128)(2,1)}), bf16[64,4,256]{2,1,0:T(4,128)(2,1)S(1)}, u32[]{:S(2)}, u32[]{:S(2)}) %all-to-all-start.4) | async-done | bytes 131104 | tf_op jit(solution)/shard_map/all_to_all | solution.py:90
  45.9 3.5 %all-to-all-start.2 = ((bf16[64,4,256]{2,1,0:T(4,128)(2,1)}), bf16[64,4,256]{2,1,0:T(4,128)(2,1)S(1)}, u32[]{:S(2)}, u32[]{:S(2)}) async-start(bf16[64,4,256]{2,1,0:T(4,128)(2,1)} %get-tuple-element.13), calls=%async_computation.2 | async-start | bytes 262144 | tf_op jit(solution)/shard_map/all_to_all | solution.py:91
  49.4 0.1 broadcast_compare_fusion
  49.5 0.1 fusion.39
  49.6 7.7 %all-to-all-done.2 = bf16[64,4,256]{2,1,0:T(4,128)(2,1)S(1)} async-done(((bf16[64,4,256]{2,1,0:T(4,128)(2,1)}), bf16[64,4,256]{2,1,0:T(4,128)(2,1)S(1)}, u32[]{:S(2)}, u32[]{:S(2)}) %all-to-all-start.2) | async-done | bytes 131104 | tf_op jit(solution)/shard_map/all_to_all | solution.py:91
  57.3 3.5 %all-to-all-start.1 = ((bf16[64,4,256]{2,1,0:T(4,128)(2,1)}), bf16[64,4,256]{2,1,0:T(4,128)(2,1)S(1)}, u32[]{:S(2)}, u32[]{:S(2)}) async-start(bf16[64,4,256]{2,1,0:T(4,128)(2,1)} %get-tuple-element.12), calls=%async_computation.1 | async-start | bytes 262144 | tf_op jit(solution)/shard_map/all_to_all | solution.py:88
  60.8 0.1 broadcast_and_fusion
  60.9 0.8 gather_fusion
  61.7 0.9 broadcast_select_fusion
  62.7 0.2 reshape.205
  62.9 0.2 reshape.206
  63.1 6.5 %all-to-all-done.1 = bf16[64,4,256]{2,1,0:T(4,128)(2,1)S(1)} async-done(((bf16[64,4,256]{2,1,0:T(4,128)(2,1)}), bf16[64,4,256]{2,1,0:T(4,128)(2,1)S(1)}, u32[]{:S(2)}, u32[]{:S(2)}) %all-to-all-start.1) | async-done | bytes 131104 | tf_op jit(solution)/shard_map/all_to_all | solution.py:88
  69.6 3.5 %all-to-all-start = ((bf16[64,4,512]{2,1,0:T(4,128)(2,1)}), bf16[64,4,512]{2,1,0:T(4,128)(2,1)S(1)}, u32[]{:S(2)}, u32[]{:S(2)}) async-start(bf16[64,4,512]{2,1,0:T(4,128)(2,1)} %broadcast_select_fusion), calls=%async_computation | async-start | bytes 524288 | tf_op jit(solution)/shard_map/all_to_all | solution.py:87
  73.1 0.3 fusion.7
  73.5 0.2 reshape.204
  73.6 0.1 fusion.46
  73.8 0.3 fusion.9
  74.1 0.2 copy.83
  74.3 0.2 concatenate.9
  74.6 9.4 %all-to-all-done = bf16[64,4,512]{2,1,0:T(4,128)(2,1)S(1)} async-done(((bf16[64,4,512]{2,1,0:T(4,128)(2,1)}), bf16[64,4,512]{2,1,0:T(4,128)(2,1)S(1)}, u32[]{:S(2)}, u32[]{:S(2)}) %all-to-all-start) | async-done | bytes 262176 | tf_op jit(solution)/shard_map/all_to_all | solution.py:87
  84.1 0.0 copy-start.3
  84.1 0.2 reshape.208
  84.3 1.4 %multiply_reduce_fusion = (f32[256]{0:T(256)S(1)}, f32[256,512]{1,0:T(8,128)S(1)}) fusion(f32[256,512]{1,0:T(8,128)S(1)} %reshape.208, bf16[512,512]{1,0:T(8,128)(2,1)} %param.17, bf16[256,256]{1,0:T(8,128)(2,1)S(1)} %concatenate.9, bf16[256,256]{1,0:T(8,128)(2,1)S(1)} %concatenate.8), kind=kOutput, calls=%fused_computation.37 | convolution fusion | flops 135134976 | bytes 1836032 | tf_op jit(solution)/shard_map/dot_general | solution.py:104
  85.7 0.0 all-gather.4.cloned.1.call-done
  85.7 1.7 %fusion.19 = f32[256,1024]{1,0:T(8,128)S(1)} fusion(bf16[512,1024]{1,0:T(8,128)(2,1)} %all-gather.4.cloned.1.call-done, f32[256,512]{1,0:T(8,128)S(1)} %get-tuple-element.17, f32[512]{0:T(512)S(1)} %copy-done.3, f32[256]{0:T(256)S(1)} %add_rsqrt_fusion.1), kind=kOutput, calls=%fused_computation.40 | convolution fusion | flops 268828672 | bytes 2624512 | tf_op jit(solution)/shard_map/dot_general | solution.py:108
  87.5 4.6 %all-gather.6.cloned.1.call-done = bf16[512,1024]{1,0:T(8,128)(2,1)} async-done(((bf16[32,1024]{1,0:T(8,128)(2,1)}), bf16[512,1024]{1,0:T(8,128)(2,1)}) %all-gather.6.cloned.1.call-update) | async-done | bytes 1048592 | tf_op jit(solution)/shard_map/all_gather | solution.py:66
  92.1 39.1 %all-gather.8.cloned.1.call-done = bf16[1024,512]{1,0:T(8,128)(2,1)} async-done(((bf16[64,512]{1,0:T(8,128)(2,1)}), bf16[1024,512]{1,0:T(8,128)(2,1)}) %all-gather.8.cloned.1.call-update) | async-done | bytes 1048592 | tf_op jit(solution)/shard_map/all_gather | solution.py:67
  131.2 2.4 %convolution_add_fusion = bf16[256,512]{1,0:T(8,128)(2,1)S(1)} fusion(f32[256,512]{1,0:T(8,128)S(1)} %get-tuple-element.17, bf16[1024,512]{1,0:T(8,128)(2,1)} %all-gather.8.cloned.1.call-done, bf16[512,1024]{1,0:T(8,128)(2,1)} %all-gather.6.cloned.1.call-done, f32[256,1024]{1,0:T(8,128)S(1)} %fusion.19, f32[512]{0:T(512)S(1)} %copy-done.3, ...), kind=kOutput, calls=%fused_computation.12 | convolution fusion | flops 539099136 | bytes 3935232 | tf_op jit(solution)/shard_map/dot_general | solution.py:111
  133.6 0.8 select_convert_fusion
  (16 shorter events, 0.3 us)
Async XLA Ops:
  6.5 4.7 %copy-start = (bf16[512,1536]{1,0:T(8,128)(2,1)S(1)}, bf16[512,1536]{1,0:T(8,128)(2,1)}, u32[]{:S(2)}) copy-start(bf16[512,1536]{1,0:T(8,128)(2,1)} %param.16) | copy-start | bytes 4718596
  6.5 79.2 %all-gather.4.cloned.1.call-start = ((), (), s32[]{:S(2)}) async-start(), calls=%async_computation.5 | async-start | bytes 1114112 | tf_op jit(solution)/shard_map/all_gather | solution.py:65
  7.3 84.8 %all-gather.6.cloned.1.call-start = ((), (), s32[]{:S(2)}) async-start(), calls=%async_computation.6 | async-start | bytes 1114112 | tf_op jit(solution)/shard_map/all_gather | solution.py:66
  13.4 0.7 copy-start.4
  14.1 35.3 %copy-start.2 = (s32[64]{0:T(128)S(1)}, s32[64]{0:T(128)}, u32[]{:S(2)}) copy-start(s32[64]{0:T(128)} %param.13) | copy-start | bytes 772
  14.8 46.1 %copy-start.1 = (bf16[64,4,512]{2,1,0:T(4,128)(2,1)S(1)}, bf16[64,4,512]{2,1,0:T(4,128)(2,1)}, u32[]{:S(2)}) copy-start(bf16[64,4,512]{2,1,0:T(4,128)(2,1)} %param.12) | copy-start | bytes 786436
  33.5 12.4 %all-to-all-start.4 = ((bf16[64,4,256]{2,1,0:T(4,128)(2,1)}), bf16[64,4,256]{2,1,0:T(4,128)(2,1)S(1)}, u32[]{:S(2)}, u32[]{:S(2)}) async-start(bf16[64,4,256]{2,1,0:T(4,128)(2,1)} %get-tuple-element.15), calls=%async_computation.4 | async-start | bytes 262144 | tf_op jit(solution)/shard_map/all_to_all | solution.py:90
  37.0 94.2 %all-gather.8.cloned.1.call-start = ((), (), s32[]{:S(2)}) async-start(), calls=%async_computation.7 | async-start | bytes 1114112 | tf_op jit(solution)/shard_map/all_gather | solution.py:67
  45.9 11.4 %all-to-all-start.2 = ((bf16[64,4,256]{2,1,0:T(4,128)(2,1)}), bf16[64,4,256]{2,1,0:T(4,128)(2,1)S(1)}, u32[]{:S(2)}, u32[]{:S(2)}) async-start(bf16[64,4,256]{2,1,0:T(4,128)(2,1)} %get-tuple-element.13), calls=%async_computation.2 | async-start | bytes 262144 | tf_op jit(solution)/shard_map/all_to_all | solution.py:91
  57.3 12.3 %all-to-all-start.1 = ((bf16[64,4,256]{2,1,0:T(4,128)(2,1)}), bf16[64,4,256]{2,1,0:T(4,128)(2,1)S(1)}, u32[]{:S(2)}, u32[]{:S(2)}) async-start(bf16[64,4,256]{2,1,0:T(4,128)(2,1)} %get-tuple-element.12), calls=%async_computation.1 | async-start | bytes 262144 | tf_op jit(solution)/shard_map/all_to_all | solution.py:88
  69.6 14.4 %all-to-all-start = ((bf16[64,4,512]{2,1,0:T(4,128)(2,1)}), bf16[64,4,512]{2,1,0:T(4,128)(2,1)S(1)}, u32[]{:S(2)}, u32[]{:S(2)}) async-start(bf16[64,4,512]{2,1,0:T(4,128)(2,1)} %broadcast_select_fusion), calls=%async_computation | async-start | bytes 524288 | tf_op jit(solution)/shard_map/all_to_all | solution.py:87
  84.1 1.7 %copy-start.3 = (f32[512]{0:T(512)S(1)}, f32[512]{0:T(512)}, u32[]{:S(2)}) copy-start(f32[512]{0:T(512)} %param.18) | copy-start | bytes 6148
Sparse Core Ops, SparseCore 0:
  9.5 42.2 all-gather.3
  54.0 38.0 all-gather.5
  94.2 36.9 all-gather.7
where the time goes:
time: 142 us; the launch traced here: 141 us
  waiting for transfers between devices  77.5 us (55%)
  blocking collectives  15.5 us (11%)
  starting transfers between devices  14.1 us (10%)
  between operations  13.4 us (9%)
  matrix products  7.24 us (5%)
  local copies, waits for them, and re-layouts  7.19 us (5%)
  other arithmetic  5.9 us (4%)
    all_gather x1, waiting for transfers between devices, per_device(): lax.all_gather(w_down, 'harm', axis=0, tiled=True)  39.1 us
    all_to_all x1, blocking collectives, per_device(): lax.all_to_all(query_rows, 'harm', split_axis=0, concat_axis=1, tiled=True)  15.5 us
    all_to_all x1, waiting for transfers between devices, per_device(): lax.all_to_all(feat_rows, 'harm', split_axis=0, concat_axis=1, tiled=True)  9.41 us
    all_to_all x1, waiting for transfers between devices, per_device(): lax.all_to_all(key_rows, 'harm', split_axis=0, concat_axis=1, tiled=True)  8.07 us
    all_to_all x1, waiting for transfers between devices, per_device(): lax.all_to_all(value_rows, 'harm', split_axis=0, concat_axis=1, tiled=True)  7.73 us
    all_to_all x1, waiting for transfers between devices, per_device(): lax.all_to_all(ell_rows, 'harm', split_axis=0, concat_axis=1, tiled=True)  6.48 us
    all_gather x1, waiting for transfers between devices, per_device(): lax.all_gather(w_up, 'harm', axis=0, tiled=True)  4.59 us
    all_to_all x1, starting transfers between devices, per_device(): lax.all_to_all(feat_rows, 'harm', split_axis=0, concat_axis=1, tiled=True)  3.53 us
  transfers between devices with their start and end apart: 7, of which 6 were waited for; matrix products, arithmetic and copies ran while one was open for 12% of the time, Pallas kernels for 0%

commit v1 on v0

--- a/solution.py
+++ b/solution.py
@@ -7,6 +7,13 @@
 WIN = 256
 eps = 1e-06
 masked = -1e30
+
+
+def swap_blocks(array, axis, split, join):
+    devices = lax.axis_size(axis)
+    shards = jnp.stack(jnp.split(array, devices, axis=split), axis=0)
+    shards = lax.all_to_all(shards, axis, split_axis=0, concat_axis=0)
+    return jnp.concatenate(shards, axis=join)
 
 
 def rms_scale(values, gain):
@@ -88,7 +95,7 @@
         lax.all_to_all(ell_rows, "harm", split_axis=0, concat_axis=1, tiled=True),
         lax.all_to_all(query_rows, "harm", split_axis=0, concat_axis=1, tiled=True),
         lax.all_to_all(key_rows, "harm", split_axis=0, concat_axis=1, tiled=True),
-        lax.all_to_all(value_rows, "harm", split_axis=0, concat_axis=1, tiled=True),
+        swap_blocks(value_rows, "harm", 0, 1),
     )
     shape_heads = (rows_here, length, half, head_dim)
     a_m = row_attention(

time: 142 us -> 143 us (level)
  blocking collectives: 15.5 us -> 0 us
  starting transfers between devices: 14.1 us -> 24 us
  local copies, waits for them, and re-layouts: 7.19 us -> 16.1 us
  waiting for transfers between devices: 77.5 us -> 75.4 us
    all_to_all x1 -> x0, blocking collectives: 15.5 us -> none  [per_device(): lax.all_to_all(query_rows, 'harm', split_axis=0, concat_axis=1, tiled=True)]
    unnamed x10 -> x25, local copies, waits for them, and re-layouts: 0.24 us -> 9.22 us
    all_to_all x1 -> x2, starting transfers between devices: 3.51 us -> 10.9 us  [the longest x1 7.36 us: per_device(): lax.all_to_all(query_rows, 'harm', split_axis=0, concat_axis=1, tiled=True)]
    all_gather x1, waiting for transfers between devices: 4.59 us -> 1.33 us  [per_device(): lax.all_gather(w_up, 'harm', axis=0, tiled=True)]
    all_to_all x1, starting transfers between devices: 3.51 us -> 6.01 us  [per_device(): lax.all_to_all(key_rows, 'harm', split_axis=0, concat_axis=1, tiled=True)]
    all_to_all x1, waiting for transfers between devices: 9.41 us -> 11 us  [per_device(): lax.all_to_all(feat_rows, 'harm', split_axis=0, concat_axis=1, tiled=True)]
    all_to_all x1 -> x2, waiting for transfers between devices: 7.73 us -> 7.78 us  [the longest x1 7.78 us: swap_blocks(): shards = lax.all_to_all(shards, axis, split_axis=0, concat_axis=0)]
  transfers between devices with their start and end apart: 7 -> 8, of which waited for: 6 -> 6; matrix products, arithmetic and copies ran while one was open for 12% -> 18% of each run, Pallas kernels for 0% -> 0%
where the time goes in v1:
time: 143 us; the launch traced here: 142 us
  waiting for transfers between devices  75.4 us (53%)
  starting transfers between devices  24 us (17%)
  local copies, waits for them, and re-layouts  16.1 us (11%)
  between operations  13.5 us (9%)
  matrix products  7.15 us (5%)
  other arithmetic  5.89 us (4%)
    all_gather x1, waiting for transfers between devices, per_device(): lax.all_gather(w_down, 'harm', axis=0, tiled=True)  40.1 us
    all_to_all x1, waiting for transfers between devices, per_device(): lax.all_to_all(feat_rows, 'harm', split_axis=0, concat_axis=1, tiled=True)  11 us
    unnamed x25, local copies, waits for them, and re-layouts  9.22 us
    all_to_all x1, waiting for transfers between devices, swap_blocks(): shards = lax.all_to_all(shards, axis, split_axis=0, concat_axis=0)  7.78 us
    all_to_all x1, waiting for transfers between devices, per_device(): lax.all_to_all(key_rows, 'harm', split_axis=0, concat_axis=1, tiled=True)  7.37 us
    all_to_all x1, starting transfers between devices, per_device(): lax.all_to_all(query_rows, 'harm', split_axis=0, concat_axis=1, tiled=True)  7.36 us
    all_to_all x1, starting transfers between devices, per_device(): lax.all_to_all(key_rows, 'harm', split_axis=0, concat_axis=1, tiled=True)  6.01 us
    all_to_all x1, waiting for transfers between devices, per_device(): lax.all_to_all(ell_rows, 'harm', split_axis=0, concat_axis=1, tiled=True)  5.72 us
  transfers between devices with their start and end apart: 8, of which 6 were waited for; matrix products, arithmetic and copies ran while one was open for 18% of the time, Pallas kernels for 0%

profile of v1, /device:TPU:0, one launch (start us, length us, event | category | flops | bytes accessed | tf_op | source)
XLA Modules:
  0.0 142.0 jit_solution(8976134450344202523)
XLA Ops:
  6.5 0.7 all-gather.4.cloned.1.call-update
  7.3 0.7 all-gather.6.cloned.1.call-update
  8.0 1.2 fusion.15
  9.2 1.2 fusion.17
  10.4 0.6 convolution_convert_fusion
  11.0 0.2 reshape.198
  11.2 0.3 fusion.44
  11.5 0.2 reshape.262
  11.7 0.2 reshape.263
  11.9 0.2 copy.114
  12.2 0.1 broadcast_and_fusion.1
  12.3 0.3 fusion.8
  12.6 0.1 fusion.45
  12.8 0.3 convolution_convert_fusion.2
  13.1 0.2 copy.120
  13.2 0.2 copy-done.4
  13.4 0.7 gather_fusion.1
  14.1 0.7 gather_fusion.2
  14.9 0.7 gather_fusion.3
  15.5 0.7 gather_fusion.4
  16.3 1.1 broadcast_select_fusion.4
  17.3 7.4 %all-to-all-start.3 = ((bf16[64,4,256]{2,1,0:T(4,128)(2,1)}), bf16[64,4,256]{2,1,0:T(4,128)(2,1)S(1)}, u32[]{:S(2)}, u32[]{:S(2)}) async-start(bf16[64,4,256]{2,1,0:T(4,128)(2,1)} %get-tuple-element.14), calls=%async_computation.3 | async-start | bytes 262144 | tf_op jit(solution)/shard_map/all_to_all | solution.py:96
  24.7 0.7 all-gather.8.cloned.1.call-update
  25.4 0.6 constant_dynamic-update-slice_fusion.15
  26.0 0.6 constant_dynamic-update-slice_fusion.14
  26.6 0.6 constant_dynamic-update-slice_fusion.13
  27.2 0.6 constant_dynamic-update-slice_fusion.12
  27.8 0.6 constant_dynamic-update-slice_fusion.11
  28.4 0.6 constant_dynamic-update-slice_fusion.10
  29.0 0.6 constant_dynamic-update-slice_fusion.9
  29.6 0.6 constant_dynamic-update-slice_fusion.8
  30.2 0.6 constant_dynamic-update-slice_fusion.7
  30.8 0.6 constant_dynamic-update-slice_fusion.6
  31.4 0.6 constant_dynamic-update-slice_fusion.5
  32.0 0.6 constant_dynamic-update-slice_fusion.4
  32.6 0.6 constant_dynamic-update-slice_fusion.3
  33.2 0.6 constant_dynamic-update-slice_fusion.2
  33.8 6.0 %all-to-all-start.4 = ((bf16[64,4,256]{2,1,0:T(4,128)(2,1)}), bf16[64,4,256]{2,1,0:T(4,128)(2,1)S(1)}, u32[]{:S(2)}, u32[]{:S(2)}) async-start(bf16[64,4,256]{2,1,0:T(4,128)(2,1)} %get-tuple-element.15), calls=%async_computation.4 | async-start | bytes 262144 | tf_op jit(solution)/shard_map/all_to_all | solution.py:97
  39.8 0.6 constant_dynamic-update-slice_fusion.1
  40.5 0.6 constant_dynamic-update-slice_fusion
  41.1 7.4 %all-to-all-done.4 = bf16[64,4,256]{2,1,0:T(4,128)(2,1)S(1)} async-done(((bf16[64,4,256]{2,1,0:T(4,128)(2,1)}), bf16[64,4,256]{2,1,0:T(4,128)(2,1)S(1)}, u32[]{:S(2)}, u32[]{:S(2)}) %all-to-all-start.4) | async-done | bytes 131104 | tf_op jit(solution)/shard_map/all_to_all | solution.py:97
  48.5 3.5 %all-to-all-start.2 = ((bf16[16,4,4,256]{3,2,1,0:T(4,128)(2,1)}), bf16[16,4,4,256]{3,2,1,0:T(4,128)(2,1)S(1)}, u32[]{:S(2)}, u32[]{:S(2)}) async-start(bf16[16,4,4,256]{3,2,1,0:T(4,128)(2,1)} %constant_dynamic-update-slice_fusion), calls=%async_computation.2 | async-start | bytes 262144 | tf_op jit(solution)/shard_map/all_to_all | solution.py:15
  52.2 7.8 %all-to-all-done.2 = bf16[16,4,4,256]{3,2,1,0:T(4,128)(2,1)S(1)} async-done(((bf16[16,4,4,256]{3,2,1,0:T(4,128)(2,1)}), bf16[16,4,4,256]{3,2,1,0:T(4,128)(2,1)S(1)}, u32[]{:S(2)}, u32[]{:S(2)}) %all-to-all-start.2) | async-done | bytes 131104 | tf_op jit(solution)/shard_map/all_to_all | solution.py:15
  59.9 3.5 %all-to-all-start.1 = ((bf16[64,4,256]{2,1,0:T(4,128)(2,1)}), bf16[64,4,256]{2,1,0:T(4,128)(2,1)S(1)}, u32[]{:S(2)}, u32[]{:S(2)}) async-start(bf16[64,4,256]{2,1,0:T(4,128)(2,1)} %get-tuple-element.12), calls=%async_computation.1 | async-start | bytes 262144 | tf_op jit(solution)/shard_map/all_to_all | solution.py:95
  63.6 0.8 gather_fusion
  64.4 0.9 broadcast_select_fusion
  65.3 0.2 reshape.204
  65.6 0.2 reshape.205
  65.8 5.7 %all-to-all-done.1 = bf16[64,4,256]{2,1,0:T(4,128)(2,1)S(1)} async-done(((bf16[64,4,256]{2,1,0:T(4,128)(2,1)}), bf16[64,4,256]{2,1,0:T(4,128)(2,1)S(1)}, u32[]{:S(2)}, u32[]{:S(2)}) %all-to-all-start.1) | async-done | bytes 131104 | tf_op jit(solution)/shard_map/all_to_all | solution.py:95
  71.5 3.5 %all-to-all-start = ((bf16[64,4,512]{2,1,0:T(4,128)(2,1)}), bf16[64,4,512]{2,1,0:T(4,128)(2,1)S(1)}, u32[]{:S(2)}, u32[]{:S(2)}) async-start(bf16[64,4,512]{2,1,0:T(4,128)(2,1)} %broadcast_select_fusion), calls=%async_computation | async-start | bytes 524288 | tf_op jit(solution)/shard_map/all_to_all | solution.py:94
  75.0 0.3 fusion.7
  75.3 0.2 reshape_reshape.3
  75.5 0.1 fusion.46
  75.7 0.3 fusion.9
  76.0 0.2 copy.129
  76.2 0.2 concatenate.9
  76.5 11.0 %all-to-all-done = bf16[64,4,512]{2,1,0:T(4,128)(2,1)S(1)} async-done(((bf16[64,4,512]{2,1,0:T(4,128)(2,1)}), bf16[64,4,512]{2,1,0:T(4,128)(2,1)S(1)}, u32[]{:S(2)}, u32[]{:S(2)}) %all-to-all-start) | async-done | bytes 262176 | tf_op jit(solution)/shard_map/all_to_all | solution.py:94
  87.5 0.2 reshape.207
  87.7 1.4 %multiply_reduce_fusion = (f32[256]{0:T(256)S(1)}, f32[256,512]{1,0:T(8,128)S(1)}) fusion(f32[256,512]{1,0:T(8,128)S(1)} %reshape.207, bf16[512,512]{1,0:T(8,128)(2,1)} %param.17, bf16[256,256]{1,0:T(8,128)(2,1)S(1)} %concatenate.9, bf16[256,256]{1,0:T(8,128)(2,1)S(1)} %concatenate.8), kind=kOutput, calls=%fused_computation.37 | convolution fusion | flops 135134976 | bytes 1836032 | tf_op jit(solution)/shard_map/dot_general | solution.py:111
  89.2 1.7 %fusion.19 = f32[256,1024]{1,0:T(8,128)S(1)} fusion(bf16[512,1024]{1,0:T(8,128)(2,1)} %all-gather.4.cloned.1.call-done, f32[256,512]{1,0:T(8,128)S(1)} %get-tuple-element.17, f32[512]{0:T(512)S(1)} %copy-done.3, f32[256]{0:T(256)S(1)} %add_rsqrt_fusion.1), kind=kOutput, calls=%fused_computation.40 | convolution fusion | flops 268828672 | bytes 2624512 | tf_op jit(solution)/shard_map/dot_general | solution.py:115
  90.9 1.3 all-gather.6.cloned.1.call-done
  92.2 40.1 %all-gather.8.cloned.1.call-done = bf16[1024,512]{1,0:T(8,128)(2,1)} async-done(((bf16[64,512]{1,0:T(8,128)(2,1)}), bf16[1024,512]{1,0:T(8,128)(2,1)}) %all-gather.8.cloned.1.call-update) | async-done | bytes 1048592 | tf_op jit(solution)/shard_map/all_gather | solution.py:74
  132.3 2.3 %convolution_add_fusion = bf16[256,512]{1,0:T(8,128)(2,1)S(1)} fusion(f32[256,512]{1,0:T(8,128)S(1)} %get-tuple-element.17, bf16[1024,512]{1,0:T(8,128)(2,1)} %all-gather.8.cloned.1.call-done, bf16[512,1024]{1,0:T(8,128)(2,1)} %all-gather.6.cloned.1.call-done, f32[256,1024]{1,0:T(8,128)S(1)} %fusion.19, f32[512]{0:T(512)S(1)} %copy-done.3, ...), kind=kOutput, calls=%fused_computation.12 | convolution fusion | flops 539099136 | bytes 3935232 | tf_op jit(solution)/shard_map/dot_general | solution.py:118
  134.7 0.8 select_convert_fusion
  (33 shorter events, 1.0 us)
Async XLA Ops:
  6.5 3.9 %copy-start = (bf16[512,1536]{1,0:T(8,128)(2,1)S(1)}, bf16[512,1536]{1,0:T(8,128)(2,1)}, u32[]{:S(2)}) copy-start(bf16[512,1536]{1,0:T(8,128)(2,1)} %param.16) | copy-start | bytes 4718596
  6.5 82.6 %all-gather.4.cloned.1.call-start = ((), (), s32[]{:S(2)}) async-start(), calls=%async_computation.5 | async-start | bytes 1114112 | tf_op jit(solution)/shard_map/all_gather | solution.py:72
  7.3 85.0 %all-gather.6.cloned.1.call-start = ((), (), s32[]{:S(2)}) async-start(), calls=%async_computation.6 | async-start | bytes 1114112 | tf_op jit(solution)/shard_map/all_gather | solution.py:73
  11.2 0.9 copy-start.2
  12.8 0.7 copy-start.4
  14.8 48.7 %copy-start.1 = (bf16[64,4,512]{2,1,0:T(4,128)(2,1)S(1)}, bf16[64,4,512]{2,1,0:T(4,128)(2,1)}, u32[]{:S(2)}) copy-start(bf16[64,4,512]{2,1,0:T(4,128)(2,1)} %param.12) | copy-start | bytes 786436
  17.3 16.5 %all-to-all-start.3 = ((bf16[64,4,256]{2,1,0:T(4,128)(2,1)}), bf16[64,4,256]{2,1,0:T(4,128)(2,1)S(1)}, u32[]{:S(2)}, u32[]{:S(2)}) async-start(bf16[64,4,256]{2,1,0:T(4,128)(2,1)} %get-tuple-element.14), calls=%async_computation.3 | async-start | bytes 262144 | tf_op jit(solution)/shard_map/all_to_all | solution.py:96
  24.7 107.7 %all-gather.8.cloned.1.call-start = ((), (), s32[]{:S(2)}) async-start(), calls=%async_computation.7 | async-start | bytes 1114112 | tf_op jit(solution)/shard_map/all_gather | solution.py:74
  33.8 14.7 %all-to-all-start.4 = ((bf16[64,4,256]{2,1,0:T(4,128)(2,1)}), bf16[64,4,256]{2,1,0:T(4,128)(2,1)S(1)}, u32[]{:S(2)}, u32[]{:S(2)}) async-start(bf16[64,4,256]{2,1,0:T(4,128)(2,1)} %get-tuple-element.15), calls=%async_computation.4 | async-start | bytes 262144 | tf_op jit(solution)/shard_map/all_to_all | solution.py:97
  48.5 11.5 %all-to-all-start.2 = ((bf16[16,4,4,256]{3,2,1,0:T(4,128)(2,1)}), bf16[16,4,4,256]{3,2,1,0:T(4,128)(2,1)S(1)}, u32[]{:S(2)}, u32[]{:S(2)}) async-start(bf16[16,4,4,256]{3,2,1,0:T(4,128)(2,1)} %constant_dynamic-update-slice_fusion), calls=%async_computation.2 | async-start | bytes 262144 | tf_op jit(solution)/shard_map/all_to_all | solution.py:15
  59.9 11.5 %all-to-all-start.1 = ((bf16[64,4,256]{2,1,0:T(4,128)(2,1)}), bf16[64,4,256]{2,1,0:T(4,128)(2,1)S(1)}, u32[]{:S(2)}, u32[]{:S(2)}) async-start(bf16[64,4,256]{2,1,0:T(4,128)(2,1)} %get-tuple-element.12), calls=%async_computation.1 | async-start | bytes 262144 | tf_op jit(solution)/shard_map/all_to_all | solution.py:95
  71.5 16.0 %all-to-all-start = ((bf16[64,4,512]{2,1,0:T(4,128)(2,1)}), bf16[64,4,512]{2,1,0:T(4,128)(2,1)S(1)}, u32[]{:S(2)}, u32[]{:S(2)}) async-start(bf16[64,4,512]{2,1,0:T(4,128)(2,1)} %broadcast_select_fusion), calls=%async_computation | async-start | bytes 524288 | tf_op jit(solution)/shard_map/all_to_all | solution.py:94
  87.5 1.7 %copy-start.3 = (f32[512]{0:T(512)S(1)}, f32[512]{0:T(512)}, u32[]{:S(2)}) copy-start(f32[512]{0:T(512)} %param.18) | copy-start | bytes 6148
Sparse Core Ops, SparseCore 0:
  9.5 41.0 all-gather.3
  52.8 39.3 all-gather.5
  94.4 37.8 all-gather.7
